TPU v7x, 32 devices: a whole 2x2x4 slice. The times are simulated.
32 devices in a mesh: ia: 2 (over y), ja: 4 (over z), ka: 4 (over x, core).
Axes of the slice: x: 2, y: 2, z: 4, core: 2. Of those that a mesh axis runs over, the one named last changes fastest.
Arguments:
- blocks: bfloat16 [256, 64, 4096], P(('ia', 'ja', 'ka')), may hold values from -12 to 12
- coords: int32 [256, 3], P(('ia', 'ja', 'ka')), may hold values from 0 to 63, as said below
- factor_one: float32 [2048, 512], P('ia'), may hold values from -1.2 to 1.2
- factor_two: float32 [4096, 512], P('ja'), may hold values from -1.2 to 1.2
- factor_three: float32 [4096, 512], P('ka'), may hold values from -1.2 to 1.2
Outputs:
- swept_one: float32 [2048, 512], P('ia')
- swept_two: float32 [4096, 512], P('ja')
- swept_three: float32 [4096, 512], P('ka')
Inputs may be any that keep to these rules, and one draw needn't show every extreme that they name: Row n of coords holds the three block coordinates of block n. The 8 rows of one device of ia+ja+ka (aligned blocks of 8 rows, devices in the order ia, ja, ka) have their second coordinate within that device's ja range (16 * ja to 16 * ja + 15) and their third within its ka range; at most 8 of them have a first coordinate within any one index of ia's range of 16; in every group of devices that share ja and ka, some index of ia receives exactly 8 from each device of the group. The same block may be listed more than once.
All inputs are finite; a program needn't handle non-finite values.
Results may differ from a plain program's by a relative error of at most 0.0028.
Values may be sent and summed in bfloat16 or wider, within the bound.
A program may use at most 64 MiB of HBM per device.

v0:
```python
import jax
import jax.numpy as jnp
from jax import lax
from jax.sharding import PartitionSpec as P

STEP_SIZE = 0.01
einsum_forms = (
    ("qk,rk->qrk", "pk,qrk->pqr", "pqr,qrk->pk"),
    ("pk,rk->prk", "qk,prk->pqr", "pqr,prk->qk"),
    ("pk,qk->pqk", "rk,pqk->pqr", "pqr,pqk->rk"),
)
other_modes = ((1, 2), (0, 2), (0, 1))


def block_gradient(cube, rows, mode):
    first, second = other_modes[mode]
    outer_form, model_form, grad_form = einsum_forms[mode]
    khatri = jnp.einsum(
        outer_form, rows[first].astype(jnp.float32), rows[second].astype(jnp.float32)
    ).astype(jnp.bfloat16)
    model = jnp.einsum(model_form, rows[mode], khatri, preferred_element_type=jnp.float32)
    misfit = (cube.astype(jnp.float32) - model).astype(jnp.bfloat16)
    return jnp.einsum(grad_form, misfit, khatri, preferred_element_type=jnp.float32)


def accumulate(blocks, coords, factors, starts, live, mode, height):
    edge = blocks.shape[1]
    width = factors[0].shape[1]

    def visit(index, total):

        def add(running):
            place = coords[index]
            rows = tuple(
                (
                    lax.dynamic_slice_in_dim(factors[f], place[f] * edge - starts[f], edge, 0)
                    for f in range(3)
                )
            )
            cube = blocks[index].reshape(edge, edge, edge)
            term = block_gradient(cube, rows, mode)
            offset = place[mode] * edge - starts[mode]
            current = lax.dynamic_slice_in_dim(running, offset, edge, 0)
            return lax.dynamic_update_slice_in_dim(running, current + term, offset, 0)

        return lax.cond(live[index], add, lambda running: running, total)

    empty = jnp.zeros((height, width), jnp.float32)
    return lax.fori_loop(0, blocks.shape[0], visit, empty)


def block_slots(coords, count, per_pair, held_rows):
    target = coords[:, 0] // held_rows
    same = target[:, None] == target[None, :]
    earlier = jnp.arange(count)[None, :] < jnp.arange(count)[:, None]
    before = jnp.sum((same & earlier).astype(jnp.int32), axis=1)
    return target * per_pair + before


def serve_rows(incoming, factor, edge, held_rows):
    width = factor.shape[1]
    within = incoming - lax.axis_index("ia") * held_rows
    safe_rows = jnp.clip(within, 0, held_rows - 1)
    picked = factor.astype(jnp.bfloat16).reshape(held_rows, edge, width)[safe_rows]
    return lax.all_to_all(picked, "ia", split_axis=0, concat_axis=0, tiled=True)


def per_device(blocks, coords, factor_one, factor_two, factor_three):
    edge = blocks.shape[1]
    count = blocks.shape[0]
    groups = lax.axis_size("ia")
    span_one = factor_one.shape[0]
    span_two = factor_two.shape[0]
    span_three = factor_three.shape[0]
    width = factor_one.shape[1]
    held_rows = span_one // edge
    per_pair = max(2, 2 * count // groups)
    start_two = lax.axis_index("ja") * span_two
    start_three = lax.axis_index("ka") * span_three
    slot = block_slots(coords, count, per_pair, held_rows)
    all_slots = groups * per_pair
    wanted = jnp.full((all_slots,), -1, jnp.int32).at[slot].set(coords[:, 0])
    incoming = lax.all_to_all(wanted, "ia", split_axis=0, concat_axis=0, tiled=True)
    fetched = serve_rows(incoming, factor_one, edge, held_rows).reshape(all_slots * edge, width)
    places = coords.at[:, 0].set(slot)
    live = jnp.ones((count,), jnp.bool_)
    slot_terms = accumulate(
        blocks,
        places,
        (fetched, factor_two.astype(jnp.bfloat16), factor_three.astype(jnp.bfloat16)),
        (0, start_two, start_three),
        live,
        0,
        all_slots * edge,
    )
    returned = lax.all_to_all(
        slot_terms.reshape(all_slots, edge, width), "ia", split_axis=0, concat_axis=0, tiled=True
    )
    within = incoming - lax.axis_index("ia") * held_rows
    selector = (within[None, :] == jnp.arange(held_rows)[:, None]).astype(jnp.float32)
    first_part = jnp.dot(
        selector,
        returned.reshape(all_slots, edge * width),
        precision=lax.Precision.HIGHEST,
        preferred_element_type=jnp.float32,
    ).reshape(span_one, width)
    first_part = lax.psum(first_part, ("ja", "ka"))
    factor_one = factor_one + STEP_SIZE * first_part
    first_rows = serve_rows(incoming, factor_one, edge, held_rows).reshape(
        groups * per_pair * edge, width
    )
    first_start = 0
    second_part = accumulate(
        blocks,
        places,
        (first_rows, factor_two.astype(jnp.bfloat16), factor_three.astype(jnp.bfloat16)),
        (first_start, start_two, start_three),
        live,
        1,
        span_two,
    )
    second_part = lax.psum(second_part, ("ia", "ka"))
    factor_two = factor_two + STEP_SIZE * second_part
    third_part = accumulate(
        blocks,
        places,
        (first_rows, factor_two.astype(jnp.bfloat16), factor_three.astype(jnp.bfloat16)),
        (first_start, start_two, start_three),
        live,
        2,
        span_three,
    )
    third_part = lax.psum(third_part, ("ia", "ja"))
    factor_three = factor_three + STEP_SIZE * third_part
    return (factor_one, factor_two, factor_three)


def solution(mesh):
    in_specs = (
        P(("ia", "ja", "ka"), None, None),
        P(("ia", "ja", "ka"), None),
        P("ia", None),
        P("ja", None),
        P("ka", None),
    )
    out_specs = (P("ia", None), P("ja", None), P("ka", None))
    return jax.shard_map(
        per_device, mesh=mesh, in_specs=in_specs, out_specs=out_specs, check_vma=False
    )
```

profile of v0, /device:TPU:0, one launch (start us, length us, event | category | flops | bytes accessed | tf_op | source)
XLA Modules:
  0.0 621.7 jit_solution(2798835930513432250)
XLA Ops:
  10.6 4.3 all-to-all-start
  27.9 8.9 %all-to-all-done.1 = bf16[16,64,512]{2,1,0:T(8,128)(2,1)S(1)} async-done(((bf16[16,64,512]{2,1,0:T(8,128)(2,1)}), bf16[16,64,512]{2,1,0:T(8,128)(2,1)S(1)}, u32[]{:S(2)}, u32[]{:S(2)}) %all-to-all-start.1) | async-done | bytes 1048608 | tf_op jit(solution)/shard_map/all_to_all | solution.py:65
  38.3 86.3 %while.40 = (s32[]{:T(128)}, f32[1024,512]{1,0:T(8,128)}, s32[8,3]{0,1:T(4,128)S(1)}, bf16[8,64,4096]{2,1,0:T(8,128)(2,1)}, bf16[1024,512]{1,0:T(8,128)(2,1)S(1)...) while((s32[]{:T(128)}, f32[1024,512]{1,0:T(8,128)}, ...), condition=%wide.region_4.5_spmd, body=%wide.region_3.4_spmd.sunk | while | flops 546144256 | bytes 15402399 | solution.py:49
  44.1 5.0 fusion.118
  54.8 5.0 fusion.118
  65.6 5.0 fusion.118
  76.4 5.0 fusion.118
  87.2 5.0 fusion.118
  98.0 5.0 fusion.118
  108.8 5.0 fusion.118
  119.6 5.0 fusion.118
  128.5 23.1 %all-to-all-done.2 = f32[16,64,512]{2,1,0:T(8,128)S(1)} async-done(((f32[16,64,512]{2,1,0:T(8,128)}), f32[16,64,512]{2,1,0:T(8,128)S(1)}, u32[]{:S(2)}, u32[]{:S(2)}) %all-to-all-start.2) | async-done | bytes 2097184 | tf_op jit(solution)/shard_map/all_to_all | solution.py:96
  155.5 98.7 %all-reduce.4.cloned.1.call-done = f32[1024,512]{1,0:T(8,128)} async-done(((f32[1024,512]{1,0:T(8,128)}), f32[1024,512]{1,0:T(8,128)}) %all-reduce.4.cloned.1.call-update) | async-done | bytes 2097168 | tf_op jit(solution)/shard_map/psum | solution.py:107
  259.3 4.4 all-to-all-start.3
  263.9 12.9 %all-to-all-done.3 = bf16[16,64,512]{2,1,0:T(8,128)(2,1)} async-done(((bf16[16,64,512]{2,1,0:T(8,128)(2,1)}), bf16[16,64,512]{2,1,0:T(8,128)(2,1)}, u32[]{:S(2)}, u32[]{:S(2)}) %all-to-all-start.3) | async-done | bytes 1048608 | tf_op jit(solution)/shard_map/all_to_all | solution.py:65
  278.4 92.2 %while.41 = (s32[]{:T(128)}, f32[1024,512]{1,0:T(8,128)}, s32[8,3]{0,1:T(4,128)S(1)}, s32[]{:T(128)}, bf16[8,64,4096]{2,1,0:T(8,128)(2,1)}, /*index=5*/s32[]{:T(...) while((s32[]{:T(128)}, f32[1024,512]{1,0:T(8,128)}, ...), condition=%wide.region_7.8_spmd, body=%wide.region_6.7_spmd.sunk | while | flops 546144256 | bytes 9110887 | solution.py:49
  285.6 4.4 fusion.123
  297.1 4.4 fusion.123
  308.6 4.4 fusion.123
  320.1 4.4 fusion.123
  331.6 4.4 fusion.123
  343.2 4.4 fusion.123
  354.7 4.4 fusion.123
  366.2 4.4 fusion.123
  370.6 59.9 %all-reduce.6.cloned.1.call-done = f32[1024,512]{1,0:T(8,128)} async-done(((f32[1024,512]{1,0:T(8,128)}), f32[1024,512]{1,0:T(8,128)}) %all-reduce.6.cloned.1.call-update) | async-done | bytes 2097168 | tf_op jit(solution)/shard_map/psum | solution.py:122
  435.6 74.6 %while.42 = (s32[]{:T(128)}, f32[1024,512]{1,0:T(8,128)}, s32[8,3]{0,1:T(4,128)S(1)}, s32[]{:T(128)}, bf16[8,64,4096]{2,1,0:T(8,128)(2,1)}, /*index=5*/s32[]{:T(...) while((s32[]{:T(128)}, f32[1024,512]{1,0:T(8,128)}, ...), condition=%wide.region_10.11_spmd, body=%wide.region_9.10_spmd.sunk | while | flops 546144256 | bytes 15402399 | solution.py:49
  469.1 3.8 fusion.128
  478.4 3.8 fusion.128
  487.7 3.8 fusion.128
  497.0 3.8 fusion.128
  506.4 3.8 fusion.128
  510.2 101.5 %all-reduce.8.cloned.1.call-done = f32[1024,512]{1,0:T(8,128)} async-done(((f32[1024,512]{1,0:T(8,128)}), f32[1024,512]{1,0:T(8,128)}) %all-reduce.8.cloned.1.call-update) | async-done | bytes 2097168 | tf_op jit(solution)/shard_map/psum | solution.py:133
  (240 shorter events, 152.5 us)
Async XLA Ops:
  10.6 8.0 %all-to-all-start = ((s32[2,8,1]{1,2,0:T(1,128)}), s32[2,8,1]{1,2,0:T(1,128)S(1)}, u32[]{:S(2)}, u32[]{:S(2)}) async-start(s32[2,8,1]{1,2,0:T(1,128)} %bitcast.29), calls=%async_computation | async-start | bytes 2048 | tf_op jit(solution)/shard_map/all_to_all | solution.py:83
  20.3 16.5 %all-to-all-start.1 = ((bf16[16,64,512]{2,1,0:T(8,128)(2,1)}), bf16[16,64,512]{2,1,0:T(8,128)(2,1)S(1)}, u32[]{:S(2)}, u32[]{:S(2)}) async-start(bf16[16,64,512]{2,1,0:T(8,128)(2,1)} %gather_fusion), calls=%async_computation.1 | async-start | bytes 2097152 | tf_op jit(solution)/shard_map/all_to_all | solution.py:65
  44.1 5.1 copy-start.7
  49.1 3.8 copy-start.6
  54.8 5.1 copy-start.7
  59.9 3.8 copy-start.6
  65.6 5.1 copy-start.7
  70.7 3.8 copy-start.6
  76.4 5.1 copy-start.7
  81.5 3.8 copy-start.6
  87.2 5.1 copy-start.7
  92.3 3.8 copy-start.6
  98.0 5.1 copy-start.7
  103.0 3.8 copy-start.6
  108.8 5.1 copy-start.7
  119.6 5.1 copy-start.7
  124.6 27.0 %all-to-all-start.2 = ((f32[16,64,512]{2,1,0:T(8,128)}), f32[16,64,512]{2,1,0:T(8,128)S(1)}, u32[]{:S(2)}, u32[]{:S(2)}) async-start(f32[16,64,512]{2,1,0:T(8,128)} %bitcast.175), calls=%async_computation.2 | async-start | bytes 4194304 | tf_op jit(solution)/shard_map/all_to_all | solution.py:96
  128.4 125.9 %all-reduce.4.cloned.1.call-start = ((), (), s32[]{:S(2)}) async-start(), calls=%async_computation.4 | async-start | bytes 4194304 | tf_op jit(solution)/shard_map/psum | solution.py:107
  155.5 98.8 %copy-start = (f32[1024,512]{1,0:T(8,128)S(1)}, f32[1024,512]{1,0:T(8,128)}, u32[]{:S(2)}) copy-start(f32[1024,512]{1,0:T(8,128)} %param.15) | copy-start | bytes 6291460
  259.3 17.6 %all-to-all-start.3 = ((bf16[16,64,512]{2,1,0:T(8,128)(2,1)}), bf16[16,64,512]{2,1,0:T(8,128)(2,1)}, u32[]{:S(2)}, u32[]{:S(2)}) async-start(bf16[16,64,512]{2,1,0:T(8,128)(2,1)} %gather_fusion.1), calls=%async_computation.3 | async-start | bytes 2097152 | tf_op jit(solution)/shard_map/all_to_all | solution.py:65
  263.7 166.9 %all-reduce.6.cloned.1.call-start = ((), (), s32[]{:S(2)}) async-start(), calls=%async_computation.5 | async-start | bytes 4194304 | tf_op jit(solution)/shard_map/psum | solution.py:122
  370.6 60.0 %copy-start.2 = (f32[1024,512]{1,0:T(8,128)S(1)}, f32[1024,512]{1,0:T(8,128)}, u32[]{:S(2)}) copy-start(f32[1024,512]{1,0:T(8,128)} %param.16) | copy-start | bytes 6291460
  370.6 241.1 %all-reduce.8.cloned.1.call-start = ((), (), s32[]{:S(2)}) async-start(), calls=%async_computation.6 | async-start | bytes 4194304 | tf_op jit(solution)/shard_map/psum | solution.py:133
  441.1 3.8 copy-start.5
  450.4 3.8 copy-start.5
  459.7 3.8 copy-start.5
  469.0 3.8 copy-start.5
  478.4 3.8 copy-start.5
  487.7 3.8 copy-start.5
  497.0 3.8 copy-start.5
  506.4 3.8 copy-start.5
  510.2 101.5 %copy-start.3 = (f32[1024,512]{1,0:T(8,128)S(1)}, f32[1024,512]{1,0:T(8,128)}, u32[]{:S(2)}) copy-start(f32[1024,512]{1,0:T(8,128)} %param.17) | copy-start | bytes 6291460
  (11 other events, 38.6 us)
Sparse Core Ops, SparseCore 0:
  155.6 98.5 all-reduce.3
  370.7 59.7 all-reduce.5
  510.3 101.3 all-reduce.7
where the time goes:
time: 626 us; the launch traced here: 622 us
  waiting for transfers between devices  307 us (49%)
  matrix products  107 us (17%)
  other arithmetic  65.5 us (10%)
  local copies, waits for them, and re-layouts  64.8 us (10%)
  loops' own time  47.1 us (8%)
  starting transfers between devices  16.3 us (3%)
  between operations  13.8 us (2%)
    dot_general x24, matrix products, block_gradient(): jnp.einsum(grad_form, misfit, khatri, preferred_element_type=jnp.float32)  106 us
    psum x1, waiting for transfers between devices, per_device(): third_part = lax.psum(third_part, ('ia', 'ja'))  102 us
    psum x1, waiting for transfers between devices, per_device(): first_part = lax.psum(first_part, ('ja', 'ka'))  98.7 us
    psum x1, waiting for transfers between devices, per_device(): second_part = lax.psum(second_part, ('ia', 'ka'))  59.9 us
    another operation x3, loops' own time, accumulate(): return lax.fori_loop(0, blocks.shape[0], visit, empty)  47.1 us
    convert_element_type x32, local copies, waits for them, and re-layouts, block_gradient(): misfit = (cube.astype(jnp.float32) - model).astype(jnp.bfloat16)  34.5 us
    convert_element_type x24, other arithmetic, block_gradient(): misfit = (cube.astype(jnp.float32) - model).astype(jnp.bfloat16)  26.8 us
    all_to_all x1, waiting for transfers between devices, per_device(): lax.all_to_all(slot_terms.reshape(all_slots, edge, width), 'ia', split_ax...  23.1 us
  transfers between devices with their start and end apart: 7, of which 7 were waited for; matrix products, arithmetic and copies ran while one was open for 1% of the time, Pallas kernels for 0%

commit v1 on v0

--- a/solution.py
+++ b/solution.py
@@ -104,7 +104,7 @@
         precision=lax.Precision.HIGHEST,
         preferred_element_type=jnp.float32,
     ).reshape(span_one, width)
-    first_part = lax.psum(first_part, ("ja", "ka"))
+    first_part = jnp.sum(lax.all_gather(first_part, ("ja", "ka")), axis=0)
     factor_one = factor_one + STEP_SIZE * first_part
     first_rows = serve_rows(incoming, factor_one, edge, held_rows).reshape(
         groups * per_pair * edge, width

time: 626 us -> 710 us (1.13)
  waiting for transfers between devices: 307 us -> 379 us
  other arithmetic: 65.5 us -> 78.3 us
    all_gather x0 -> x1, waiting for transfers between devices: none -> 169 us  [per_device(): first_part = jnp.sum(lax.all_gather(first_part, ('ja', 'ka')), axis=0)]
    psum x1 -> x0, waiting for transfers between devices: 98.7 us -> none  [per_device(): first_part = lax.psum(first_part, ('ja', 'ka'))]
    reduce_sum x0 -> x1, other arithmetic: none -> 12.7 us  [per_device(): first_part = jnp.sum(lax.all_gather(first_part, ('ja', 'ka')), axis=0)]
where the time goes in v1:
time: 710 us; the launch traced here: 706 us
  waiting for transfers between devices  379 us (53%)
  matrix products  107 us (15%)
  other arithmetic  78.3 us (11%)
  local copies, waits for them, and re-layouts  64.9 us (9%)
  loops' own time  46.6 us (7%)
  starting transfers between devices  16.3 us (2%)
  between operations  13.8 us (2%)
    all_gather x1, waiting for transfers between devices, per_device(): first_part = jnp.sum(lax.all_gather(first_part, ('ja', 'ka')), axis=0)  169 us
    dot_general x24, matrix products, block_gradient(): jnp.einsum(grad_form, misfit, khatri, preferred_element_type=jnp.float32)  106 us
    psum x1, waiting for transfers between devices, per_device(): third_part = lax.psum(third_part, ('ia', 'ja'))  102 us
    psum x1, waiting for transfers between devices, per_device(): second_part = lax.psum(second_part, ('ia', 'ka'))  60.9 us
    another operation x3, loops' own time, accumulate(): return lax.fori_loop(0, blocks.shape[0], visit, empty)  46.6 us
    convert_element_type x32, local copies, waits for them, and re-layouts, block_gradient(): misfit = (cube.astype(jnp.float32) - model).astype(jnp.bfloat16)  34.5 us
    convert_element_type x24, other arithmetic, block_gradient(): misfit = (cube.astype(jnp.float32) - model).astype(jnp.bfloat16)  26.8 us
    all_to_all x1, waiting for transfers between devices, per_device(): lax.all_to_all(slot_terms.reshape(all_slots, edge, width), 'ia', split_ax...  23.1 us
  transfers between devices with their start and end apart: 7, of which 7 were waited for; matrix products, arithmetic and copies ran while one was open for 1% of the time, Pallas kernels for 0%

profile of v1, /device:TPU:0, one launch (start us, length us, event | category | flops | bytes accessed | tf_op | source)
XLA Modules:
  0.0 706.1 jit_solution(1299535961271233969)
XLA Ops:
  10.6 4.3 all-to-all-start
  27.9 8.9 %all-to-all-done.1 = bf16[16,64,512]{2,1,0:T(8,128)(2,1)S(1)} async-done(((bf16[16,64,512]{2,1,0:T(8,128)(2,1)}), bf16[16,64,512]{2,1,0:T(8,128)(2,1)S(1)}, u32[]{:S(2)}, u32[]{:S(2)}) %all-to-all-start.1) | async-done | bytes 1048608 | tf_op jit(solution)/shard_map/all_to_all | solution.py:65
  38.3 84.5 %while.40 = (s32[]{:T(128)}, f32[1024,512]{1,0:T(8,128)}, s32[8,3]{0,1:T(4,128)S(1)}, bf16[8,64,4096]{2,1,0:T(8,128)(2,1)}, bf16[1024,512]{1,0:T(8,128)(2,1)S(1)...) while((s32[]{:T(128)}, f32[1024,512]{1,0:T(8,128)}, ...), condition=%wide.region_4.5_spmd, body=%wide.region_3.4_spmd.sunk | while | flops 546144256 | bytes 15402391 | solution.py:49
  43.8 5.0 fusion.118
  54.4 5.0 fusion.118
  65.0 5.0 fusion.118
  75.5 5.0 fusion.118
  86.1 5.0 fusion.118
  96.7 5.0 fusion.118
  107.3 5.0 fusion.118
  117.8 5.0 fusion.118
  126.8 23.1 %all-to-all-done.2 = f32[16,64,512]{2,1,0:T(8,128)S(1)} async-done(((f32[16,64,512]{2,1,0:T(8,128)}), f32[16,64,512]{2,1,0:T(8,128)S(1)}, u32[]{:S(2)}, u32[]{:S(2)}) %all-to-all-start.2) | async-done | bytes 2097184 | tf_op jit(solution)/shard_map/all_to_all | solution.py:96
  153.8 168.5 %all-gather.2.cloned.1.call-done = f32[16,1024,512]{2,1,0:T(8,128)} async-done(((f32[1,1024,512]{2,1,0:T(8,128)}), f32[16,1024,512]{2,1,0:T(8,128)}) %all-gather.2.cloned.1.call-update) | async-done | bytes 33554448 | tf_op jit(solution)/shard_map/all_gather | solution.py:107
  322.3 12.7 %reduce_sum.22 = f32[1024,512]{1,0:T(8,128)S(1)} reduce(f32[16,1024,512]{2,1,0:T(8,128)} %all-gather.2.cloned.1.call-done, f32[]{:T(128)} %constant.179.clone.1), dimensions={0}, to_apply=%region_5.6 | reduce | flops 7864320 | bytes 35651588 | tf_op jit(solution)/shard_map/reduce_sum | solution.py:107
  340.0 4.4 all-to-all-start.3
  344.7 14.1 %all-to-all-done.3 = bf16[16,64,512]{2,1,0:T(8,128)(2,1)} async-done(((bf16[16,64,512]{2,1,0:T(8,128)(2,1)}), bf16[16,64,512]{2,1,0:T(8,128)(2,1)}, u32[]{:S(2)}, u32[]{:S(2)}) %all-to-all-start.3) | async-done | bytes 1048608 | tf_op jit(solution)/shard_map/all_to_all | solution.py:65
  360.4 93.1 %while.41 = (s32[]{:T(128)}, f32[1024,512]{1,0:T(8,128)}, s32[8,3]{0,1:T(4,128)S(1)}, s32[]{:T(128)}, bf16[8,64,4096]{2,1,0:T(8,128)(2,1)}, /*index=5*/s32[]{:T(...) while((s32[]{:T(128)}, f32[1024,512]{1,0:T(8,128)}, ...), condition=%wide.region_7.8_spmd, body=%wide.region_6.7_spmd.sunk | while | flops 546144256 | bytes 9110879 | solution.py:49
  367.7 4.4 fusion.123
  379.3 4.4 fusion.123
  391.0 4.4 fusion.123
  402.6 4.4 fusion.123
  414.2 4.4 fusion.123
  425.9 4.4 fusion.123
  437.5 4.4 fusion.123
  449.2 4.4 fusion.123
  453.6 60.9 %all-reduce.3.cloned.1.call-done = f32[1024,512]{1,0:T(8,128)} async-done(((f32[1024,512]{1,0:T(8,128)}), f32[1024,512]{1,0:T(8,128)}) %all-reduce.3.cloned.1.call-update) | async-done | bytes 2097168 | tf_op jit(solution)/shard_map/psum | solution.py:122
  519.5 75.0 %while.42 = (s32[]{:T(128)}, f32[1024,512]{1,0:T(8,128)}, s32[8,3]{0,1:T(4,128)S(1)}, s32[]{:T(128)}, bf16[8,64,4096]{2,1,0:T(8,128)(2,1)}, /*index=5*/s32[]{:T(...) while((s32[]{:T(128)}, f32[1024,512]{1,0:T(8,128)}, ...), condition=%wide.region_10.11_spmd, body=%wide.region_9.10_spmd.sunk | while | flops 546144256 | bytes 15402391 | solution.py:49
  534.5 3.8 fusion.128
  553.2 3.8 fusion.128
  562.6 3.8 fusion.128
  581.4 3.8 fusion.128
  594.6 101.5 %all-reduce.5.cloned.1.call-done = f32[1024,512]{1,0:T(8,128)} async-done(((f32[1024,512]{1,0:T(8,128)}), f32[1024,512]{1,0:T(8,128)}) %all-reduce.5.cloned.1.call-update) | async-done | bytes 2097168 | tf_op jit(solution)/shard_map/psum | solution.py:133
  (239 shorter events, 156.5 us)
Async XLA Ops:
  10.6 8.0 %all-to-all-start = ((s32[2,8,1]{1,2,0:T(1,128)}), s32[2,8,1]{1,2,0:T(1,128)S(1)}, u32[]{:S(2)}, u32[]{:S(2)}) async-start(s32[2,8,1]{1,2,0:T(1,128)} %bitcast.29), calls=%async_computation | async-start | bytes 2048 | tf_op jit(solution)/shard_map/all_to_all | solution.py:83
  20.3 16.5 %all-to-all-start.1 = ((bf16[16,64,512]{2,1,0:T(8,128)(2,1)}), bf16[16,64,512]{2,1,0:T(8,128)(2,1)S(1)}, u32[]{:S(2)}, u32[]{:S(2)}) async-start(bf16[16,64,512]{2,1,0:T(8,128)(2,1)} %gather_fusion), calls=%async_computation.1 | async-start | bytes 2097152 | tf_op jit(solution)/shard_map/all_to_all | solution.py:65
  43.8 5.1 copy-start.6
  54.4 5.1 copy-start.6
  65.0 5.1 copy-start.6
  75.5 5.1 copy-start.6
  86.1 5.1 copy-start.6
  96.7 5.1 copy-start.6
  107.2 5.1 copy-start.6
  117.8 5.1 copy-start.6
  122.9 27.0 %all-to-all-start.2 = ((f32[16,64,512]{2,1,0:T(8,128)}), f32[16,64,512]{2,1,0:T(8,128)S(1)}, u32[]{:S(2)}, u32[]{:S(2)}) async-start(f32[16,64,512]{2,1,0:T(8,128)} %bitcast.174), calls=%async_computation.2 | async-start | bytes 4194304 | tf_op jit(solution)/shard_map/all_to_all | solution.py:96
  126.6 195.7 %all-gather.2.cloned.1.call-start = ((), (), s32[]{:S(2)}) async-start(), calls=%async_computation.4 | async-start | bytes 35651584 | tf_op jit(solution)/shard_map/all_gather | solution.py:107
  340.0 18.8 %all-to-all-start.3 = ((bf16[16,64,512]{2,1,0:T(8,128)(2,1)}), bf16[16,64,512]{2,1,0:T(8,128)(2,1)}, u32[]{:S(2)}, u32[]{:S(2)}) async-start(bf16[16,64,512]{2,1,0:T(8,128)(2,1)} %gather_fusion.1), calls=%async_computation.3 | async-start | bytes 2097152 | tf_op jit(solution)/shard_map/all_to_all | solution.py:65
  344.5 170.1 %all-reduce.3.cloned.1.call-start = ((), (), s32[]{:S(2)}) async-start(), calls=%async_computation.5 | async-start | bytes 4194304 | tf_op jit(solution)/shard_map/psum | solution.py:122
  453.5 61.0 %copy-start.1 = (f32[1024,512]{1,0:T(8,128)S(1)}, f32[1024,512]{1,0:T(8,128)}, u32[]{:S(2)}) copy-start(f32[1024,512]{1,0:T(8,128)} %param.16) | copy-start | bytes 6291460
  453.6 242.6 %all-reduce.5.cloned.1.call-start = ((), (), s32[]{:S(2)}) async-start(), calls=%async_computation.6 | async-start | bytes 4194304 | tf_op jit(solution)/shard_map/psum | solution.py:133
  525.1 3.8 copy-start.4
  528.9 3.6 copy-start.3
  534.5 3.8 copy-start.4
  538.3 3.6 copy-start.3
  543.8 3.8 copy-start.4
  547.7 3.6 copy-start.3
  553.2 3.8 copy-start.4
  557.1 3.6 copy-start.3
  562.6 3.8 copy-start.4
  566.4 3.6 copy-start.3
  572.0 3.8 copy-start.4
  575.8 3.6 copy-start.3
  581.4 3.8 copy-start.4
  585.2 3.6 copy-start.3
  590.8 3.8 copy-start.4
  594.6 101.6 %copy-start.2 = (f32[1024,512]{1,0:T(8,128)S(1)}, f32[1024,512]{1,0:T(8,128)}, u32[]{:S(2)}) copy-start(f32[1024,512]{1,0:T(8,128)} %param.17) | copy-start | bytes 6291460
  (10 other events, 34.8 us)
Sparse Core Ops, SparseCore 0:
  153.9 168.3 all-gather.1
  453.7 60.8 all-reduce.2
  594.7 101.3 all-reduce.4
